TPU v7x, 256 devices: a whole 4x4x8 slice. The times are simulated.
256 devices in a mesh: pair: 64 (over y, z, core), aux: 4 (over x).
Axes of the slice: x: 4, y: 4, z: 8, core: 2. Of those that a mesh axis runs over, the one named last changes fastest.
Arguments:
- factors: bfloat16 [64, 8192, 8, 128], P('pair', 'aux'), may hold values from -0.0625 to 0.0625
- amplitudes: bfloat16 [3072, 128, 128], P('pair'), may hold values from -6 to 6
- block_list: int32 [3072, 3], P('pair'), may hold values from 0 to 63, as said below
- owner_map: int32 [64], replicated, may hold values from 0 to 63, as said below
Outputs:
- residual_blocks: bfloat16 [3072, 128, 128], P('pair')
Inputs may be any that keep to these rules, and one draw needn't show every extreme that they name: `block_list`: each row (k, A, C) names an occupied orbital below 64 and two virtual blocks below 8; no row repeats. Among the 48 rows of one device at most 2 have orbitals with the same owner_map entry, and exactly 2 for some entry on every device. `owner_map`: A permutation: entry k is the row of factors that holds orbital k.
All inputs are finite; a program needn't handle non-finite values.
Results may differ from a plain program's by a relative error of at most 0.0046.
Values may be sent and summed in bfloat16 or wider, within the bound.
A program may use at most 64 MiB of HBM per device.

v0:
```python
import jax
import jax.numpy as jnp
from jax import lax
from jax.sharding import PartitionSpec as P

CAP = 2


def on_device(factors, amplitudes, block_list, owner_map):
    pair_count = lax.axis_size("pair")
    slot_total = pair_count * CAP
    block_count = amplitudes.shape[0]
    block_width = amplitudes.shape[1]
    virt_blocks = factors.shape[2]
    share_rows = factors.shape[1]
    orbital_total = owner_map.shape[0]
    orbitals = block_list[:, 0]
    block_a = block_list[:, 1]
    block_c = block_list[:, 2]
    matches = orbitals[:, None] == lax.iota(jnp.int32, orbital_total)[None, :]
    owners = jnp.sum(jnp.where(matches, owner_map[None, :], 0), axis=1)
    owner_hits = (owners[:, None] == lax.iota(jnp.int32, pair_count)[None, :]).astype(jnp.int32)
    earlier = jnp.cumsum(owner_hits, axis=0) - owner_hits
    slot_rank = jnp.sum(earlier * owner_hits, axis=1)
    slots = owners * CAP + slot_rank
    placing = slots[:, None] == lax.iota(jnp.int32, slot_total)[None, :]
    place_matrix = placing.astype(jnp.bfloat16)
    flat_blocks = amplitudes.reshape(block_count, block_width * block_width)
    send_blocks = jnp.einsum(
        "js,jm->sm", place_matrix, flat_blocks, preferred_element_type=jnp.float32
    )
    send_blocks = send_blocks.astype(jnp.bfloat16).reshape(
        pair_count, CAP, block_width, block_width
    )
    send_a = jnp.sum(jnp.where(placing, block_a[:, None] + 1, 0), axis=0)
    send_c = jnp.sum(jnp.where(placing, block_c[:, None] + 1, 0), axis=0)
    send_index = (
        jnp.stack([send_a, send_c], axis=-1).astype(jnp.bfloat16).reshape(pair_count, CAP, 2)
    )
    recv_blocks, recv_index = (
        lax.all_to_all(send_blocks, "pair", split_axis=0, concat_axis=0, tiled=True),
        lax.all_to_all(send_index, "pair", split_axis=0, concat_axis=0, tiled=True),
    )
    recv_index = recv_index.reshape(slot_total, 2).astype(jnp.int32) - 1
    slot_a = recv_index[:, 0]
    slot_c = recv_index[:, 1]
    onehot_a = (slot_a[:, None] == lax.iota(jnp.int32, virt_blocks)[None, :]).astype(jnp.bfloat16)
    onehot_c = (slot_c[:, None] == lax.iota(jnp.int32, virt_blocks)[None, :]).astype(jnp.bfloat16)
    combined = (onehot_c[:, :, None] * onehot_a[:, None, :]).reshape(
        slot_total, virt_blocks * virt_blocks
    )
    recv_flat = recv_blocks.reshape(slot_total, block_width * block_width)
    weights = jnp.einsum("sm,sn->mn", combined, recv_flat, preferred_element_type=jnp.float32)
    weights = weights.reshape(virt_blocks, virt_blocks, block_width, block_width)
    weights = jnp.transpose(weights, (0, 3, 1, 2)).reshape(
        virt_blocks * block_width, virt_blocks * block_width
    )
    weights = weights.astype(jnp.bfloat16)
    factor_flat = factors.reshape(share_rows, virt_blocks * block_width)
    factor_rows = factor_flat
    inter_share = lax.psum_scatter(
        jnp.dot(factor_rows, weights, preferred_element_type=jnp.float32),
        "pair",
        scatter_dimension=0,
        tiled=True,
    )
    inter_share = inter_share.astype(jnp.bfloat16)
    shard_rows = lax.all_gather(inter_share, "pair", axis=0, tiled=True)
    height = shard_rows.shape[0]
    factor_rows = factor_flat
    left = shard_rows.reshape(height, virt_blocks, block_width)
    right = factor_rows.reshape(height, virt_blocks, block_width)
    projected = jnp.einsum("qAa,qCc->ACac", left, right, preferred_element_type=jnp.float32)
    safe_a = jnp.maximum(slot_a, 0)
    safe_c = jnp.maximum(slot_c, 0)
    summed = lax.psum(projected, "aux")
    picked = summed[safe_a, safe_c].astype(jnp.bfloat16)
    picked = picked.reshape(pair_count, CAP, block_width, block_width)
    returned = lax.all_to_all(picked, "pair", split_axis=0, concat_axis=0, tiled=True)
    returned = returned.reshape(slot_total, block_width * block_width)
    result = jnp.einsum("js,sm->jm", place_matrix, returned, preferred_element_type=jnp.float32)
    return result.astype(jnp.bfloat16).reshape(block_count, block_width, block_width)


def solution(mesh):
    placed = (P("pair", "aux", None, None), P("pair", None, None), P("pair", None), P())
    return jax.shard_map(
        on_device, mesh=mesh, in_specs=placed, out_specs=P("pair", None, None), check_vma=False
    )
```

profile of v0, /device:TPU:1, one launch (start us, length us, event | category | flops | bytes accessed | tf_op | source)
XLA Modules:
  0.0 617.8 jit_solution(2545537378293932037)
XLA Ops:
  6.5 0.8 add_bitcast_fusion
  7.3 0.8 select_reduce_fusion.3
  8.3 0.2 select_reduce_fusion.2
  8.7 0.1 stack.10
  8.8 0.2 stack.9
  9.0 0.7 copy.26
  9.6 13.2 %all-to-all-start = ((bf16[64,2,2]{1,2,0:T(2,128)(2,1)}), bf16[64,2,2]{1,2,0:T(2,128)(2,1)S(1)}, u32[]{:S(2)}, u32[]{:S(2)}) async-start(bf16[64,2,2]{1,2,0:T(2,128)(2,1)} %copy.26), calls=%async_computation | async-start | bytes 65536 | tf_op jit(solution)/shard_map/all_to_all | solution.py:42
  22.8 2.8 fusion.10
  25.6 3.2 copy.39
  28.8 3.2 all-to-all-done
  32.0 7.3 %all-to-all-start.1 = ((bf16[64,2,128,128]{3,2,1,0:T(8,128)(2,1)}), bf16[64,2,128,128]{3,2,1,0:T(8,128)(2,1)}, u32[]{:S(2)}, u32[]{:S(2)}) async-start(bf16[64,2,128,128]{3,2,1,0:T(8,128)(2,1)} %bitcast.84), calls=%async_computation.1 | async-start | bytes 8388608 | tf_op jit(solution)/shard_map/all_to_all | solution.py:41
  39.3 0.2 reduce-scatter.4.cloned.1.call-start
  39.7 0.1 copy.28
  39.8 0.1 sub.11
  40.0 95.3 %all-to-all-done.1 = bf16[64,2,128,128]{3,2,1,0:T(8,128)(2,1)} async-done(((bf16[64,2,128,128]{3,2,1,0:T(8,128)(2,1)}), bf16[64,2,128,128]{3,2,1,0:T(8,128)(2,1)}, u32[]{:S(2)}, u32[]{:S(2)}) %all-to-all-start.1) | async-done | bytes 4194336 | tf_op jit(solution)/shard_map/all_to_all | solution.py:41
  135.2 7.7 %copy.70 = bf16[16,8,128,128]{3,1,2,0:T(8,128)(2,1)} copy(bf16[16,8,128,128]{3,2,1,0:T(8,128)(2,1)} %bitcast.39) | data formatting | bytes 8388608
  142.9 6.4 %copy.29 = bf16[128,16384]{0,1:T(8,128)(2,1)} copy(bf16[128,16384]{1,0:T(8,128)(2,1)} %bitcast.88) | data formatting | bytes 8388608 | tf_op jit(solution)/shard_map/reshape | solution.py:52
  149.3 3.8 convert_bitcast_fusion
  153.1 3.3 copy.30
  156.3 10.6 %convolution_bitcast_fusion = f32[2048,1024]{0,1:T(8,128)} fusion(bf16[256,8,8,128]{3,2,1,0:T(8,128)(2,1)} %bitcast.92, bf16[128,8,8,128]{3,2,1,0:T(8,128)(2,1)} %bitcast.90), kind=kOutput, calls=%fused_computation.3 | convolution fusion | flops 4294967296 | bytes 14680064 | tf_op jit(solution)/shard_map/dot_general | solution.py:62
  166.9 9.3 %copy.36 = f32[2048,1024]{1,0:T(8,128)} copy(f32[2048,1024]{0,1:T(8,128)} %convolution_bitcast_fusion) | data formatting | bytes 16777216
  176.2 0.3 all-gather.2.cloned.1.call-start
  176.5 143.6 %reduce-scatter.4.cloned.1.call-done = f32[32,1024]{1,0:T(8,128)} async-done(((f32[2048,1024]{1,0:T(8,128)}), f32[32,1024]{1,0:T(8,128)}) %reduce-scatter.4.cloned.1.call-update) | async-done | bytes 131088 | tf_op jit(solution)/shard_map/reduce_scatter | solution.py:61
  320.2 1.5 convert_element_type.57
  321.7 83.6 %all-gather.2.cloned.1.call-done = bf16[2048,1024]{1,0:T(8,128)(2,1)} async-done(((bf16[32,1024]{1,0:T(8,128)(2,1)}), bf16[2048,1024]{1,0:T(8,128)(2,1)}) %all-gather.2.cloned.1.call-update) | async-done | bytes 4194320 | tf_op jit(solution)/shard_map/all_gather | solution.py:68
  405.3 6.5 %copy.32 = bf16[2048,1024]{0,1:T(8,128)(2,1)} copy(bf16[2048,1024]{1,0:T(8,128)(2,1)} %all-gather.2.cloned.1.call-done) | data formatting | bytes 8388608 | tf_op jit(solution)/shard_map/all_gather | solution.py:68
  411.8 9.9 %fusion.7 = f32[8,8,128,128]{3,2,1,0:T(8,128)} fusion(bf16[2048,8,128,1]{0,2,3,1:T(8,128)(2,1)} %bitcast.89, bf16[2048,8,128]{2,1,0:T(8,128)(2,1)} %bitcast.93), kind=kOutput, calls=%fused_computation.12 | convolution fusion | flops 4294967296 | bytes 12582912 | tf_op jit(solution)/shard_map/qAa,qCc->ACac/dot_general | solution.py:73
  421.7 78.1 %all-reduce.1 = bf16[8,8,128,128]{3,2,1,0:T(8,128)(2,1)S(1)} all-reduce(f32[8,8,128,128]{3,2,1,0:T(8,128)} %fusion.7), channel_id=1, replica_groups=mesh['pair'=64,'aux'=4] {'aux'}, use_global_device_ids=true, to_apply=%region_6.7 | all-reduce | flops 1048576 | bytes 6291456 | tf_op jit(solution)/shard_map/psum | solution.py:76
  499.8 3.1 gather_fusion
  502.8 103.9 %all_to_all.15 = bf16[64,2,128,128]{3,2,1,0:T(8,128)(2,1)S(1)} all-to-all(bf16[64,2,128,128]{3,2,1,0:T(8,128)(2,1)} %bitcast.86), channel_id=1, replica_groups=mesh['pair'=64,'aux'=4] {'pair'}, dimensions={0} | all-to-all | bytes 8388608 | tf_op jit(solution)/shard_map/all_to_all | solution.py:79
  606.7 2.7 fusion.15
  609.4 1.6 copy.44
  (13 shorter events, 0.4 us)
Async XLA Ops:
  9.6 22.4 %all-to-all-start = ((bf16[64,2,2]{1,2,0:T(2,128)(2,1)}), bf16[64,2,2]{1,2,0:T(2,128)(2,1)S(1)}, u32[]{:S(2)}, u32[]{:S(2)}) async-start(bf16[64,2,2]{1,2,0:T(2,128)(2,1)} %copy.26), calls=%async_computation | async-start | bytes 65536 | tf_op jit(solution)/shard_map/all_to_all | solution.py:42
  32.0 103.2 %all-to-all-start.1 = ((bf16[64,2,128,128]{3,2,1,0:T(8,128)(2,1)}), bf16[64,2,128,128]{3,2,1,0:T(8,128)(2,1)}, u32[]{:S(2)}, u32[]{:S(2)}) async-start(bf16[64,2,128,128]{3,2,1,0:T(8,128)(2,1)} %bitcast.84), calls=%async_computation.1 | async-start | bytes 8388608 | tf_op jit(solution)/shard_map/all_to_all | solution.py:41
  39.3 280.8 %reduce-scatter.4.cloned.1.call-start = ((), (), s32[]{:S(2)}) async-start(), calls=%async_computation.5 | async-start | bytes 8519680 | tf_op jit(solution)/shard_map/reduce_scatter | solution.py:61
  176.2 229.1 %all-gather.2.cloned.1.call-start = ((), (), s32[]{:S(2)}) async-start(), calls=%async_computation.4 | async-start | bytes 4259840 | tf_op jit(solution)/shard_map/all_gather | solution.py:68
Sparse Core Ops, SparseCore 0:
  176.4 143.7 reduce-scatter.3
  323.3 81.9 all-gather.1
where the time goes:
time: 619 us; the launch traced here: 618 us
  waiting for transfers between devices  326 us (53%)
  blocking collectives  182 us (29%)
  local copies, waits for them, and re-layouts  42.2 us (7%)
  matrix products  29.8 us (5%)
  starting transfers between devices  21 us (3%)
  between operations  13.5 us (2%)
    reduce_scatter x1, waiting for transfers between devices, on_device(): lax.psum_scatter(jnp.dot(factor_rows, weights, preferred_element_type=jnp...  144 us
    all_to_all x1, blocking collectives, on_device(): lax.all_to_all(picked, 'pair', split_axis=0, concat_axis=0, tiled=True)  104 us
    all_to_all x1, waiting for transfers between devices, on_device(): lax.all_to_all(send_blocks, 'pair', split_axis=0, concat_axis=0, tiled=True)  95.3 us
    all_gather x1, waiting for transfers between devices, on_device(): shard_rows = lax.all_gather(inter_share, 'pair', axis=0, tiled=True)  83.6 us
    psum x1, blocking collectives, on_device(): summed = lax.psum(projected, 'aux')  78.1 us
    unnamed x4, local copies, waits for them, and re-layouts  21.7 us
    all_to_all x1, starting transfers between devices, on_device(): lax.all_to_all(send_index, 'pair', split_axis=0, concat_axis=0, tiled=True)  13.2 us
  transfers between devices with their start and end apart: 4, of which 4 were waited for; matrix products, arithmetic and copies ran while one was open for 1% of the time, Pallas kernels for 0%

commit v1 on v0

--- a/solution.py
+++ b/solution.py
@@ -65,7 +65,9 @@
         tiled=True,
     )
     inter_share = inter_share.astype(jnp.bfloat16)
-    shard_rows = lax.all_gather(inter_share, "pair", axis=0, tiled=True)
+    shard_rows = jnp.concatenate(
+        lax.all_to_all(jnp.stack([inter_share] * lax.axis_size("pair")), "pair", 0, 0), axis=0
+    )
     height = shard_rows.shape[0]
     factor_rows = factor_flat
     left = shard_rows.reshape(height, virt_blocks, block_width)

time: 619 us -> 635 us (1.026)
  blocking collectives: 182 us -> 290 us
  waiting for transfers between devices: 326 us -> 242 us
    all_to_all x0 -> x1, blocking collectives: none -> 108 us  [on_device(): lax.all_to_all(jnp.stack([inter_share] * lax.axis_size('pair')), 'pair',...]
    all_gather x1 -> x0, waiting for transfers between devices: 83.6 us -> none  [on_device(): shard_rows = lax.all_gather(inter_share, 'pair', axis=0, tiled=True)]
    all_gather x1 -> x0, local copies, waits for them, and re-layouts: 6.49 us -> none  [on_device(): shard_rows = lax.all_gather(inter_share, 'pair', axis=0, tiled=True)]
    unnamed x4 -> x7, local copies, waits for them, and re-layouts: 21.7 us -> 23.9 us
  transfers between devices with their start and end apart: 4 -> 3, of which waited for: 4 -> 3; matrix products, arithmetic and copies ran while one was open for 1% -> 1% of each run, Pallas kernels for 0% -> 0%
where the time goes in v1:
time: 635 us; the launch traced here: 634 us
  blocking collectives  290 us (46%)
  waiting for transfers between devices  242 us (38%)
  local copies, waits for them, and re-layouts  38.4 us (6%)
  matrix products  25.9 us (4%)
  starting transfers between devices  20.7 us (3%)
  between operations  13.5 us (2%)
    reduce_scatter x1, waiting for transfers between devices, on_device(): lax.psum_scatter(jnp.dot(factor_rows, weights, preferred_element_type=jnp...  144 us
    all_to_all x1, blocking collectives, on_device(): lax.all_to_all(jnp.stack([inter_share] * lax.axis_size('pair')), 'pair',...  108 us
    all_to_all x1, blocking collectives, on_device(): lax.all_to_all(picked, 'pair', split_axis=0, concat_axis=0, tiled=True)  104 us
    all_to_all x1, waiting for transfers between devices, on_device(): lax.all_to_all(send_blocks, 'pair', split_axis=0, concat_axis=0, tiled=True)  95.3 us
    psum x1, blocking collectives, on_device(): summed = lax.psum(projected, 'aux')  77.7 us
    unnamed x7, local copies, waits for them, and re-layouts  23.9 us
    all_to_all x1, starting transfers between devices, on_device(): lax.all_to_all(send_index, 'pair', split_axis=0, concat_axis=0, tiled=True)  13.2 us
  transfers between devices with their start and end apart: 3, of which 3 were waited for; matrix products, arithmetic and copies ran while one was open for 1% of the time, Pallas kernels for 0%

profile of v1, /device:TPU:1, one launch (start us, length us, event | category | flops | bytes accessed | tf_op | source)
XLA Modules:
  0.0 633.7 jit_solution(1588690074056042719)
XLA Ops:
  6.5 0.8 add_bitcast_fusion
  7.3 0.8 select_reduce_fusion.3
  8.3 0.2 select_reduce_fusion.2
  8.7 0.1 stack.9
  8.8 0.2 stack.8
  9.0 0.7 copy.28
  9.6 13.2 %all-to-all-start = ((bf16[64,2,2]{1,2,0:T(2,128)(2,1)}), bf16[64,2,2]{1,2,0:T(2,128)(2,1)S(1)}, u32[]{:S(2)}, u32[]{:S(2)}) async-start(bf16[64,2,2]{1,2,0:T(2,128)(2,1)} %copy.28), calls=%async_computation | async-start | bytes 65536 | tf_op jit(solution)/shard_map/all_to_all | solution.py:42
  22.8 2.8 fusion.13
  25.6 3.2 copy.43
  28.8 3.2 all-to-all-done
  32.0 7.3 %all-to-all-start.1 = ((bf16[64,2,128,128]{3,2,1,0:T(8,128)(2,1)}), bf16[64,2,128,128]{3,2,1,0:T(8,128)(2,1)}, u32[]{:S(2)}, u32[]{:S(2)}) async-start(bf16[64,2,128,128]{3,2,1,0:T(8,128)(2,1)} %bitcast.83), calls=%async_computation.1 | async-start | bytes 8388608 | tf_op jit(solution)/shard_map/all_to_all | solution.py:41
  39.3 0.2 reduce-scatter.4.cloned.1.call-start
  39.8 0.1 sub.11
  40.0 95.3 %all-to-all-done.1 = bf16[64,2,128,128]{3,2,1,0:T(8,128)(2,1)} async-done(((bf16[64,2,128,128]{3,2,1,0:T(8,128)(2,1)}), bf16[64,2,128,128]{3,2,1,0:T(8,128)(2,1)}, u32[]{:S(2)}, u32[]{:S(2)}) %all-to-all-start.1) | async-done | bytes 4194336 | tf_op jit(solution)/shard_map/all_to_all | solution.py:41
  135.2 7.7 %copy.79 = bf16[16,8,128,128]{3,1,2,0:T(8,128)(2,1)} copy(bf16[16,8,128,128]{3,2,1,0:T(8,128)(2,1)} %bitcast.35) | data formatting | bytes 8388608
  142.9 6.4 %copy.31 = bf16[128,16384]{0,1:T(8,128)(2,1)} copy(bf16[128,16384]{1,0:T(8,128)(2,1)} %bitcast.87) | data formatting | bytes 8388608 | tf_op jit(solution)/shard_map/reshape | solution.py:52
  149.3 3.8 convert_bitcast_fusion
  153.1 3.3 copy.32
  156.3 10.6 %convolution_bitcast_fusion = f32[2048,1024]{0,1:T(8,128)} fusion(bf16[256,8,8,128]{3,2,1,0:T(8,128)(2,1)} %bitcast.92, bf16[128,8,8,128]{3,2,1,0:T(8,128)(2,1)} %bitcast.90), kind=kOutput, calls=%fused_computation.3 | convolution fusion | flops 4294967296 | bytes 14680064 | tf_op jit(solution)/shard_map/dot_general | solution.py:62
  166.9 9.3 %copy.40 = f32[2048,1024]{1,0:T(8,128)} copy(f32[2048,1024]{0,1:T(8,128)} %convolution_bitcast_fusion) | data formatting | bytes 16777216
  176.2 143.9 %reduce-scatter.4.cloned.1.call-done = f32[32,1024]{1,0:T(8,128)} async-done(((f32[2048,1024]{1,0:T(8,128)}), f32[32,1024]{1,0:T(8,128)}) %reduce-scatter.4.cloned.1.call-update) | async-done | bytes 131088 | tf_op jit(solution)/shard_map/reduce_scatter | solution.py:61
  320.2 0.9 convert_element_type.57
  321.1 0.5 stack.11
  321.6 107.9 %all_to_all.20 = bf16[64,32,1024]{2,1,0:T(8,128)(2,1)S(1)} all-to-all(bf16[64,32,1024]{2,1,0:T(8,128)(2,1)S(1)} %stack.11), channel_id=1, replica_groups=mesh['pair'=64,'aux'=4] {'pair'}, dimensions={0} | all-to-all | bytes 8388608 | tf_op jit(solution)/shard_map/all_to_all | solution.py:69
  429.5 1.1 copy.47
  430.7 1.0 copy-done
  431.7 6.1 fusion.8
  437.8 77.7 %all-reduce.1 = bf16[8,8,128,128]{3,2,1,0:T(8,128)(2,1)S(1)} all-reduce(f32[8,8,128,128]{3,2,1,0:T(8,128)} %fusion.8), channel_id=1, replica_groups=mesh['pair'=64,'aux'=4] {'aux'}, use_global_device_ids=true, to_apply=%region_6.7 | all-reduce | flops 1048576 | bytes 6291456 | tf_op jit(solution)/shard_map/psum | solution.py:78
  515.4 3.1 gather_fusion
  518.5 104.1 %all_to_all.21 = bf16[64,2,128,128]{3,2,1,0:T(8,128)(2,1)S(1)} all-to-all(bf16[64,2,128,128]{3,2,1,0:T(8,128)(2,1)} %bitcast.85), channel_id=1, replica_groups=mesh['pair'=64,'aux'=4] {'pair'}, dimensions={0} | all-to-all | bytes 8388608 | tf_op jit(solution)/shard_map/all_to_all | solution.py:81
  622.6 2.7 fusion.18
  625.3 1.6 copy.49
  (14 shorter events, 0.5 us)
Async XLA Ops:
  9.6 22.4 %all-to-all-start = ((bf16[64,2,2]{1,2,0:T(2,128)(2,1)}), bf16[64,2,2]{1,2,0:T(2,128)(2,1)S(1)}, u32[]{:S(2)}, u32[]{:S(2)}) async-start(bf16[64,2,2]{1,2,0:T(2,128)(2,1)} %copy.28), calls=%async_computation | async-start | bytes 65536 | tf_op jit(solution)/shard_map/all_to_all | solution.py:42
  32.0 103.2 %all-to-all-start.1 = ((bf16[64,2,128,128]{3,2,1,0:T(8,128)(2,1)}), bf16[64,2,128,128]{3,2,1,0:T(8,128)(2,1)}, u32[]{:S(2)}, u32[]{:S(2)}) async-start(bf16[64,2,128,128]{3,2,1,0:T(8,128)(2,1)} %bitcast.83), calls=%async_computation.1 | async-start | bytes 8388608 | tf_op jit(solution)/shard_map/all_to_all | solution.py:41
  39.3 280.8 %reduce-scatter.4.cloned.1.call-start = ((), (), s32[]{:S(2)}) async-start(), calls=%async_computation.5 | async-start | bytes 8519680 | tf_op jit(solution)/shard_map/reduce_scatter | solution.py:61
  429.5 2.2 copy-start
Sparse Core Ops, SparseCore 0:
  176.4 143.7 reduce-scatter.3
